TPU v7x, 768 devices: a whole 4x8x12 slice. The times are simulated.
768 devices in a mesh: rows: 96 (over z, x, core), grp: 8 (over y).
Axes of the slice: x: 4, y: 8, z: 12, core: 2. Of those that a mesh axis runs over, the one named last changes fastest.
Arguments:
- user_factors: bfloat16 [393216, 512], P(('rows', 'grp')), may hold values from -6 to 6
- item_factors: bfloat16 [2048, 512], P('grp'), may hold values from -0.25 to 0.25
- obs_user: int32 [6144], P(('rows', 'grp')), may hold values from 0 to 3
- obs_item: int32 [6144], P(('rows', 'grp')), may hold values from 0 to 15, as said below
- obs_weight: bfloat16 [6144, 128, 128], P(('rows', 'grp')), may hold values from 0.5 to 8
- obs_target: bfloat16 [6144, 128, 128], P(('rows', 'grp')), may hold values from -6 to 6
Outputs:
- user_grad: float32 [393216, 512], P(('rows', 'grp'))
- item_grad: float32 [2048, 512], P('grp')
Inputs may be any that keep to these rules, and one draw needn't show every extreme that they name: `obs_item`: the item tiles of one device's 8 observed tiles are all different.
All inputs are finite; a program needn't handle non-finite values.
Results may differ from a plain program's by a relative error of at most 0.0014.
Values may be sent and summed in bfloat16 or wider, within the bound.
A program may use at most 32 MiB of HBM per device.

v0:
```python
import jax
import jax.numpy as jnp
from jax import lax
from jax.sharding import PartitionSpec as P


def local(user_factors, item_factors, obs_user, obs_item, obs_weight, obs_target):
    tile = obs_weight.shape[1]
    width = user_factors.shape[1]
    item_table = lax.all_gather(item_factors, "grp", axis=0, tiled=True)
    tile_count = item_table.shape[0] // tile
    user_tiles_here = user_factors.shape[0] // tile
    item_tiles = item_table.reshape(tile_count, tile, width)
    user_tiles = user_factors.reshape(user_tiles_here, tile, width)
    user_picked = user_tiles[obs_user]
    item_picked = item_tiles[obs_item]
    predicted = jnp.einsum(
        "kuf,kif->kui", user_picked, item_picked, preferred_element_type=jnp.float32
    )
    residual = (
        obs_weight.astype(jnp.float32) * (predicted - obs_target.astype(jnp.float32)) / 16.0
    ).astype(jnp.bfloat16)
    item_terms = jnp.einsum(
        "kui,kuf->kif", residual, user_picked, preferred_element_type=jnp.float32
    ).astype(jnp.bfloat16)
    user_part = jnp.einsum(
        "kui,kif->kuf", residual, item_picked, preferred_element_type=jnp.float32
    )
    user_onehot = (
        obs_user[:, None] == jnp.arange(user_tiles_here, dtype=jnp.int32)[None, :]
    ).astype(jnp.float32)
    user_terms = jnp.einsum(
        "kb,kuf->buf", user_onehot, user_part, precision=lax.Precision.HIGHEST
    ).reshape(user_factors.shape[0], width)
    gram_items = jnp.einsum("if,ig->fg", item_table, item_table, preferred_element_type=jnp.float32)
    user_wide = user_factors.astype(jnp.float32)
    user_grad = (
        user_terms
        + 0.05 * jnp.dot(user_wide, gram_items, precision=lax.Precision.HIGHEST)
        + 0.1 * user_wide
    )
    item_onehot = (obs_item[:, None] == jnp.arange(tile_count, dtype=jnp.int32)[None, :]).astype(
        jnp.float32
    )
    dense_terms = jnp.einsum(
        "kb,kif->bif", item_onehot, item_terms.astype(jnp.float32), precision=lax.Precision.HIGHEST
    ).reshape(tile_count * tile, width)
    owned_sum = lax.psum_scatter(dense_terms, "grp", scatter_dimension=0, tiled=True)
    item_wide = item_factors.astype(jnp.float32)
    total_sum = lax.psum(owned_sum, "rows")
    item_grad = total_sum / 32.0 + 0.1 * item_wide
    return (user_grad, item_grad)


def solution(mesh):
    placed = (
        P(("rows", "grp"), None),
        P("grp", None),
        P(("rows", "grp")),
        P(("rows", "grp")),
        P(("rows", "grp"), None, None),
        P(("rows", "grp"), None, None),
    )
    return jax.shard_map(
        local,
        mesh=mesh,
        in_specs=placed,
        out_specs=(P(("rows", "grp"), None), P("grp", None)),
        check_vma=False,
    )
```

profile of v0, /device:TPU:1, one launch (start us, length us, event | category | flops | bytes accessed | tf_op | source)
XLA Modules:
  0.0 414.8 jit_solution(13098357129882271849)
XLA Ops:
  7.2 0.0 all-gather.2.cloned.1.call-start
  7.2 0.7 all-gather.2.cloned.1.call-update
  7.9 0.0 reduce-scatter.2.cloned.1.call-start
  8.0 0.7 compare_select_fusion.1
  8.6 1.7 gather_fusion
  10.4 50.2 %all-gather.2.cloned.1.call-done = bf16[2048,512]{1,0:T(8,128)(2,1)} async-done(((bf16[256,512]{1,0:T(8,128)(2,1)}), bf16[2048,512]{1,0:T(8,128)(2,1)}) %all-gather.2.cloned.1.call-update) | async-done | bytes 2097168 | tf_op jit(solution)/shard_map/all_gather | solution.py:10
  60.6 2.2 gather_fusion.1
  62.8 0.4 fusion.7
  63.3 0.5 fusion.17
  63.8 0.9 fusion.8
  64.7 4.4 %copy.13 = f32[16,128,512]{2,1,0:T(8,128)} copy(f32[16,128,512]{2,0,1:T(8,128)S(1)} %fusion.8) | data formatting | bytes 8388608 | tf_op jit(solution)/shard_map/kb,kif->bif/dot_general | solution.py:45
  69.1 0.0 all-reduce.2.cloned.1.call-start
  69.2 1.0 copy-done
  70.1 0.2 copy.12
  70.3 0.4 fusion.15
  70.8 2.2 fusion
  73.0 0.3 copy.10
  73.3 0.3 copy.11
  73.7 4.5 %fusion.16 = f32[512,512]{1,0:T(8,128)} fusion(bf16[2048,512]{1,0:T(8,128)(2,1)} %all-gather.2.cloned.1.call-done), kind=kOutput, calls=%fused_computation.26 | convolution fusion | flops 1073741824 | bytes 3145728 | tf_op jit(solution)/shard_map/if,ig->fg/dot_general | solution.py:35
  78.1 54.4 %reduce-scatter.2.cloned.1.call-done = f32[256,512]{1,0:T(8,128)} async-done(((f32[2048,512]{1,0:T(8,128)}), f32[256,512]{1,0:T(8,128)}) %reduce-scatter.2.cloned.1.call-update) | async-done | bytes 524304 | tf_op jit(solution)/shard_map/reduce_scatter | solution.py:48
  132.5 3.1 fusion.4
  135.7 1.3 copy.14
  137.0 269.4 %all-reduce.2.cloned.1.call-done = f32[256,512]{1,0:T(8,128)} async-done(((f32[256,512]{1,0:T(8,128)}), f32[256,512]{1,0:T(8,128)}) %all-reduce.2.cloned.1.call-update) | async-done | bytes 524304 | tf_op jit(solution)/shard_map/psum | solution.py:50
  406.4 1.9 multiply_add_fusion
  (16 shorter events, 0.1 us)
Async XLA Ops:
  7.2 3.2 copy-start.5
  7.2 53.4 %all-gather.2.cloned.1.call-start = ((), (), s32[]{:S(2)}) async-start(), calls=%async_computation.1 | async-start | bytes 2359296 | tf_op jit(solution)/shard_map/all_gather | solution.py:10
  7.9 124.6 %reduce-scatter.2.cloned.1.call-start = ((), (), s32[]{:S(2)}) async-start(), calls=%async_computation.2 | async-start | bytes 4718592 | tf_op jit(solution)/shard_map/reduce_scatter | solution.py:48
  8.6 54.2 %copy-start.2 = (bf16[8,128,128]{2,1,0:T(8,128)(2,1)S(1)}, bf16[8,128,128]{2,1,0:T(8,128)(2,1)}, u32[]{:S(2)}) copy-start(bf16[8,128,128]{2,1,0:T(8,128)(2,1)} %param.11) | copy-start | bytes 786436
  8.6 54.2 %copy-start.3 = (bf16[8,128,128]{2,1,0:T(8,128)(2,1)S(1)}, bf16[8,128,128]{2,1,0:T(8,128)(2,1)}, u32[]{:S(2)}) copy-start(bf16[8,128,128]{2,1,0:T(8,128)(2,1)} %param.10) | copy-start | bytes 786436
  69.1 1.0 copy-start
  69.1 1.6 copy-start.4
  69.1 337.2 %all-reduce.2.cloned.1.call-start = ((), (), s32[]{:S(2)}) async-start(), calls=%async_computation.3 | async-start | bytes 1048576 | tf_op jit(solution)/shard_map/psum | solution.py:50
  135.6 270.7 %copy-start.1 = (bf16[256,512]{1,0:T(8,128)(2,1)S(1)}, bf16[256,512]{1,0:T(8,128)(2,1)}, u32[]{:S(2)}) copy-start(bf16[256,512]{1,0:T(8,128)(2,1)} %param.7) | copy-start | bytes 786436
Sparse Core Ops, SparseCore 0:
  10.4 50.1 all-gather.1
  69.2 63.2 reduce-scatter.1
  136.1 270.2 all-reduce.1
where the time goes:
time: 415 us
  waiting for transfers between devices  375 us (90%)
  between operations  13.9 us (3%)
  matrix products  12 us (3%)
  local copies, waits for them, and re-layouts  11.5 us (3%)
    psum x1, waiting for transfers between devices, local(): total_sum = lax.psum(owned_sum, 'rows')  269 us
    reduce_scatter x1, waiting for transfers between devices, local(): lax.psum_scatter(dense_terms, 'grp', scatter_dimension=0, tiled=True)  54.4 us
    all_gather x1, waiting for transfers between devices, local(): item_table = lax.all_gather(item_factors, 'grp', axis=0, tiled=True)  50.2 us
  transfers between devices with their start and end apart: 3, of which 3 were waited for; matrix products, arithmetic and copies ran while one was open for 4% of the time, Pallas kernels for 0%

commit v1 on v0

v1 whole, which is shorter than its diff:
```python
import jax
import jax.numpy as jnp
from jax import lax
from jax.experimental import pallas as pl
from jax.experimental.pallas import tpu as pltpu
from jax.sharding import PartitionSpec as P

MESH = pl.DeviceIdType.MESH
NX, NY, NZ = 4, 8, 12
STEPS = [0, -1, 1, -2, 2, -3, 3, 4]
F32 = jnp.float32
BF16 = jnp.bfloat16


def dot(a, b, ca, cb):
    return lax.dot_general(a, b, (((ca,), (cb,)), ((), ())), preferred_element_type=F32)


def kernel(
    obs_user, obs_item, u_hbm, v_hbm, w_hbm, t_hbm, ug_hbm, is_hbm,
    uv, vt, wv, tv, tb, xr, ys, yr, q, zr, z1, tr, ob, rm, gh, ug,
    sem_in, sem_out, ag_s, ag_r, sb_s, sb_r, x_s, x_r, y_s, y_r, z_s, z_r, g_s, g_r,
):
    r = lax.axis_index("rows")
    y = lax.axis_index("grp")
    c = lax.rem(r, 2)
    x = lax.rem(r // 2, NX)
    z = r // (2 * NX)
    i, g = lax.rem(z, 4), z // 4

    def dev(dx=0, dy=0, di=0, dg=0, dc=0):
        cc = 1 - c if dc else c
        xx = lax.rem(x + dx, NX)
        zz = lax.rem(g + dg, 3) * 4 + lax.rem(i + di, 4)
        return ((zz * NX + xx) * 2 + cc, lax.rem(y + dy + NY, NY))

    def yat(d):
        return lax.rem(y + STEPS[d] + NY, NY)

    def remote(src, dst, s, t, to):
        return pltpu.make_async_remote_copy(src, dst, s, t, device_id=to, device_id_type=MESH)

    loads = [
        pltpu.make_async_copy(v_hbm, vt.at[pl.ds(2 * y, 2)], sem_in.at[0]),
        pltpu.make_async_copy(u_hbm, uv, sem_in.at[1]),
        pltpu.make_async_copy(w_hbm, wv, sem_in.at[2]),
        pltpu.make_async_copy(t_hbm, tv, sem_in.at[3]),
    ]
    for cp in loads:
        cp.start()

    peers = [dev(dy=d) for d in range(1, NY)]
    peers += [dev(dx=dx, dc=dc) for dx in range(NX) for dc in range(2) if dx or dc]
    peers += [dev(di=d) for d in range(1, 4)] + [dev(dg=d) for d in range(1, 3)]
    barrier = pltpu.get_barrier_semaphore()
    for p in peers:
        pl.semaphore_signal(barrier, inc=1, device_id=p, device_id_type=MESH)
    for cp in loads:
        cp.wait()
    pl.semaphore_wait(barrier, len(peers))

    pending = []

    def ag(direction, step, h):
        sgn = 1 if direction == 0 else -1
        src_y = lax.rem(y - sgn * (step - 1) + NY, NY)
        ref = vt.at[2 * src_y + c, h]
        k = (direction * 4 + step - 1) * 2 + h
        return remote(ref, ref, ag_s.at[k], ag_r.at[k], dev(dy=sgn))

    def ag_has(direction, step, h):
        return step < 4 or h == direction

    def to_sibling(d, h):
        ref = vt.at[2 * yat(d) + c, h]
        return remote(ref, ref, sb_s.at[d * 2 + h], sb_r.at[d * 2 + h], dev(dc=1))

    def tile(d, dc):
        yy = yat(d)
        cc = 1 - c if dc else c
        b = 2 * yy + cc
        k = jnp.int32(0)
        scale = F32(0.0)
        for n in range(8):
            hit = obs_item[n] == b
            k = jnp.where(hit, n, k)
            scale = jnp.where(hit, F32(0.0625), scale)
        j = obs_user[k]
        uk = uv[j]
        vb = vt[b].reshape(128, 512)
        predicted = dot(uk, vb, 1, 1)
        res = (wv[k].astype(F32) * (predicted - tv[k].astype(F32)) * scale).astype(BF16)
        tb[d, dc] = dot(res, uk, 0, 0).astype(BF16).reshape(4, 32, 512)
        for jj in range(4):
            keep = jnp.where(j == jj, F32(1.0), F32(0.0)).astype(BF16)
            rm[b, jj] = res * keep
        for dx in range(NX):
            if dx or dc:
                e = dx * 2 + dc
                cp = remote(
                    tb.at[d, dc, lax.rem(x + dx, NX)], xr.at[d, e],
                    x_s.at[d * 8 + e], x_r.at[d * 8 + e], dev(dx=dx, dc=dc),
                )
                cp.start()
                pending.append(cp)

    def reduce_x(d):
        total = tb[d, 0, x].astype(F32)
        for e in range(1, 8):
            remote(xr.at[d, e], xr.at[d, e], x_s.at[d * 8 + e], x_r.at[d * 8 + e], dev(dc=1)).wait_recv()
            total = total + xr[d, e].astype(F32)
        if d == 0:
            yr[0] = total
        else:
            ys[d] = total
            cp = remote(ys.at[d], yr.at[d], y_s.at[d], y_r.at[d], dev(dy=STEPS[d]))
            cp.start()
            pending.append(cp)

    for direction in range(2):
        for h in range(2):
            cp = ag(direction, 1, h)
            cp.start()
            pending.append(cp)
    tile(0, 0)
    tile(0, 1)
    for step in range(1, 5):
        here = [2 * step - 1, 2 * step] if step < 4 else [7, 7]
        for h in range(2):
            for direction in range(2):
                if not ag_has(direction, step, h):
                    continue
                ag(direction, step, h).wait_recv()
                if step < 4 and ag_has(direction, step + 1, h):
                    cp = ag(direction, step + 1, h)
                    cp.start()
                    pending.append(cp)
                cp = to_sibling(here[direction], h)
                cp.start()
                pending.append(cp)
        ds = here if step < 4 else [7]
        for d in ds:
            tile(d, 0)
        for d in ds:
            for h in range(2):
                to_sibling(d, h).wait_recv()
            tile(d, 1)
        if step == 1:
            reduce_x(0)
        else:
            for d in [2 * step - 3, 2 * step - 2]:
                reduce_x(d)
    reduce_x(7)

    table = vt[...].reshape(2048, 512)
    gram = 0.05 * dot(table, table, 0, 0)
    hi = gram.astype(BF16)
    gh[0] = hi
    rest = gram - hi.astype(F32)
    mid = rest.astype(BF16)
    gh[1] = mid
    gh[2] = (rest - mid.astype(F32)).astype(BF16)

    total = yr[0]
    for d in range(1, 8):
        remote(yr.at[d], yr.at[d], y_s.at[d], y_r.at[d], dev(dc=1)).wait_recv()
        total = total + yr[d]
    q[...] = total.reshape(4, 8, 512)
    for d in range(1, 4):
        cp = remote(q.at[lax.rem(i + d, 4)], zr.at[d], z_s.at[d], z_r.at[d], dev(di=d))
        cp.start()
        pending.append(cp)

    def user(j):
        uj = uv[j]
        acc = 0.1 * uj.astype(F32)
        for n in range(3):
            acc = acc + dot(uj, gh[n], 1, 0)
        for b in range(16):
            acc = acc + dot(rm[b, j], vt[b].reshape(128, 512), 1, 0)
        ug[j] = acc
        cp = pltpu.make_async_copy(ug.at[j], ug_hbm.at[j], sem_out.at[j])
        cp.start()
        return cp

    outs = [user(0), user(1)]

    total = q[i]
    for d in range(1, 4):
        remote(zr.at[d], zr.at[d], z_s.at[d], z_r.at[d], dev(dc=1)).wait_recv()
        total = total + zr[d]
    z1[...] = total
    for d in range(1, 3):
        cp = remote(z1, tr.at[g], z_s.at[3 + d], z_r.at[3 + d], dev(dg=d))
        cp.start()
        pending.append(cp)
    tr[g] = total
    outs += [user(2), user(3)]
    for d in range(1, 3):
        remote(z1, z1, z_s.at[3 + d], z_r.at[3 + d], dev(dc=1)).wait_recv()
    ob[c, x, i] = tr[0] + tr[1] + tr[2]

    def spread(ref, k, to):
        return remote(ref, ref, g_s.at[k], g_r.at[k], to)

    for d in range(1, 4):
        cp = spread(ob.at[c, x, i], d, dev(di=d))
        cp.start()
        pending.append(cp)
    for d in range(1, 4):
        spread(ob.at[c, x, i], d, dev(di=d)).wait_recv()
    for d in range(1, 4):
        cp = spread(ob.at[c, x], 4 + d, dev(dx=d))
        cp.start()
        pending.append(cp)
    cp = spread(ob.at[c, x], 8, dev(dc=1))
    cp.start()
    pending.append(cp)
    for d in range(1, 4):
        ref = ob.at[c, lax.rem(x + NX - d, NX)]
        spread(ref, 4 + d, dev(dx=d)).wait_recv()
        cp = spread(ref, 8 + d, dev(dc=1))
        cp.start()
        pending.append(cp)
    for d in range(4):
        spread(ob.at[c, x], 8 + d, dev(dc=1)).wait_recv()
    cp = pltpu.make_async_copy(ob, is_hbm, sem_out.at[4])
    cp.start()
    outs.append(cp)
    for cp in pending:
        cp.wait_send()
    for cp in outs:
        cp.wait()


def local(user_factors, item_factors, obs_user, obs_item, obs_weight, obs_target):
    anyspace = pl.BlockSpec(memory_space=pl.ANY)
    smem = pl.BlockSpec(memory_space=pltpu.SMEM)
    dma = pltpu.SemaphoreType.DMA
    user_grad, item_sum = pl.pallas_call(
        kernel,
        out_shape=(
            jax.ShapeDtypeStruct((4, 128, 512), F32),
            jax.ShapeDtypeStruct((2, 4, 4, 8, 512), F32),
        ),
        in_specs=[smem, smem, anyspace, anyspace, anyspace, anyspace],
        out_specs=(anyspace, anyspace),
        scratch_shapes=[
            pltpu.VMEM((4, 128, 512), BF16),
            pltpu.VMEM((16, 2, 64, 512), BF16),
            pltpu.VMEM((8, 128, 128), BF16),
            pltpu.VMEM((8, 128, 128), BF16),
            pltpu.VMEM((8, 2, 4, 32, 512), BF16),
            pltpu.VMEM((8, 8, 32, 512), BF16),
            pltpu.VMEM((8, 32, 512), F32),
            pltpu.VMEM((8, 32, 512), F32),
            pltpu.VMEM((4, 8, 512), F32),
            pltpu.VMEM((4, 8, 512), F32),
            pltpu.VMEM((8, 512), F32),
            pltpu.VMEM((3, 8, 512), F32),
            pltpu.VMEM((2, 4, 4, 8, 512), F32),
            pltpu.VMEM((16, 4, 128, 128), BF16),
            pltpu.VMEM((3, 512, 512), BF16),
            pltpu.VMEM((4, 128, 512), F32),
            dma((4,)), dma((5,)),
            dma((16,)), dma((16,)),
            dma((16,)), dma((16,)),
            dma((64,)), dma((64,)),
            dma((8,)), dma((8,)),
            dma((8,)), dma((8,)),
            dma((16,)), dma((16,)),
        ],
        compiler_params=pltpu.CompilerParams(
            collective_id=0, has_side_effects=True, vmem_limit_bytes=48 << 20
        ),
    )(
        obs_user,
        obs_item,
        user_factors.reshape(4, 128, 512),
        item_factors.reshape(2, 2, 64, 512),
        obs_weight,
        obs_target,
    )
    item_grad = item_sum.reshape(256, 512) / 32.0 + 0.1 * item_factors.astype(F32)
    return user_grad.reshape(512, 512), item_grad


def solution(mesh):
    both = P(("rows", "grp"))
    placed = (
        P(("rows", "grp"), None),
        P("grp", None),
        both,
        both,
        P(("rows", "grp"), None, None),
        P(("rows", "grp"), None, None),
    )
    return jax.shard_map(
        local,
        mesh=mesh,
        in_specs=placed,
        out_specs=(P(("rows", "grp"), None), P("grp", None)),
        check_vma=False,
    )
```

time: 415 us -> 82.1 us (0.20)
  waiting for transfers between devices: 375 us -> 0 us
  Pallas kernels: 0 us -> 74.7 us
  between operations: 13.9 us -> 0.67 us
  matrix products: 12 us -> 0 us
  local copies, waits for them, and re-layouts: 11.5 us -> 5.51 us
    psum x1 -> x0, waiting for transfers between devices: 269 us -> none  [local(): total_sum = lax.psum(owned_sum, 'rows')]
    pallas_call x0 -> x1, Pallas kernels: none -> 74.7 us  [local(): pl.pallas_call(kernel, out_shape=(jax.ShapeDtypeStruct((4, 128, 512), F32...]
    reduce_scatter x1 -> x0, waiting for transfers between devices: 54.4 us -> none  [local(): lax.psum_scatter(dense_terms, 'grp', scatter_dimension=0, tiled=True)]
    all_gather x1 -> x0, waiting for transfers between devices: 50.2 us -> none  [local(): item_table = lax.all_gather(item_factors, 'grp', axis=0, tiled=True)]
    dot_general x7 -> x0, matrix products: 12 us -> none  [the longest x1 4.47 us: local(): jnp.einsum('if,ig->fg', item_table, item_table, preferred_element_type=jn...]
    dot_general x2 -> x0, local copies, waits for them, and re-layouts: 4.72 us -> none  [the longest x1 4.38 us: local(): jnp.einsum('kb,kif->bif', item_onehot, item_terms.astype(jnp.float32), pr...]
  transfers between devices with their start and end apart: 3 -> 0, of which waited for: 3 -> 0; matrix products, arithmetic and copies ran while one was open for 4% -> 0% of each run, Pallas kernels for 0% -> 0%
where the time goes in v1:
time: 82.1 us; the launch traced here: 81.8 us
  Pallas kernels  74.7 us (91%)
  local copies, waits for them, and re-layouts  5.51 us (7%)
  other arithmetic  0.91 us (1%)
    pallas_call x1, Pallas kernels, local(): pl.pallas_call(kernel, out_shape=(jax.ShapeDtypeStruct((4, 128, 512), F32...  74.7 us
    unnamed x13, local copies, waits for them, and re-layouts  5.51 us

profile of v1, /device:TPU:1, one launch (start us, length us, event | category | flops | bytes accessed | tf_op | source)
XLA Modules:
  0.0 81.8 jit_solution(6453186176792276714)
XLA Ops:
  0.6 0.0 copy-start.4
  0.6 0.0 copy-start.5
  0.7 0.6 copy-done.4
  1.3 0.0 copy-done.5
  1.3 0.0 copy-start
  1.3 0.9 %copy-done = bf16[256,512]{1,0:T(8,128)(2,1)S(1)} copy-done((bf16[256,512]{1,0:T(8,128)(2,1)S(1)}, bf16[256,512]{1,0:T(8,128)(2,1)}, u32[]{:S(2)}) %copy-start) | copy-done | bytes 262168
  2.3 0.0 copy-start.1
  2.3 1.0 %copy-done.1 = bf16[512,512]{1,0:T(8,128)(2,1)S(1)} copy-done((bf16[512,512]{1,0:T(8,128)(2,1)S(1)}, bf16[512,512]{1,0:T(8,128)(2,1)}, u32[]{:S(2)}) %copy-start.1) | copy-done | bytes 524312
  3.3 0.0 copy-start.2
  3.3 0.9 %copy-done.2 = bf16[8,128,128]{2,1,0:T(8,128)(2,1)S(1)} copy-done((bf16[8,128,128]{2,1,0:T(8,128)(2,1)S(1)}, bf16[8,128,128]{2,1,0:T(8,128)(2,1)}, u32[]{:S(2)}) %copy-start.2) | copy-done | bytes 262168
  4.2 0.0 copy-start.3
  4.2 0.9 %copy-done.3 = bf16[8,128,128]{2,1,0:T(8,128)(2,1)S(1)} copy-done((bf16[8,128,128]{2,1,0:T(8,128)(2,1)S(1)}, bf16[8,128,128]{2,1,0:T(8,128)(2,1)}, u32[]{:S(2)}) %copy-start.3) | copy-done | bytes 262168
  5.2 74.7 %shard_map.77 = (f32[4,128,512]{2,1,0:T(8,128)S(1)}, f32[2,4,4,8,512]{4,3,2,1,0:T(8,128)S(1)}) custom-call(s32[8]{0:T(128)S(1)} %copy-done.4, s32[8]{0:T(128)S(1)} %copy-done.5, bf16[4,128,512]{2,1,0:T(8,128)(2,1)S(1)} %bitcast.7, bf16[2,2,64,512]{3,2,1,0:T(8,128)(2,1)S(1)} %bitcast.6, bf16[8,128,128]{2,1,0:T(8,128)(2,1)S(1)} %copy-done.2, ...), custom_call_target="tpu_custom_call" | custom-call | tf_op jit(solution)/shard_map/pallas_call | solution.py:240
  79.9 0.9 %bitcast_add_fusion = f32[256,512]{1,0:T(8,128)} fusion(f32[2,4,4,8,512]{4,3,2,1,0:T(8,128)S(1)} %broadcast_multiply_fusion, bf16[256,512]{1,0:T(8,128)(2,1)S(1)} %copy-done), kind=kLoop, calls=%fused_computation | loop fusion | flops 393216 | bytes 1310720 | tf_op jit(solution)/shard_map/add | solution.py:284
  80.8 1.0 %copy.9 = f32[512,512]{1,0:T(8,128)} copy(f32[512,512]{1,0:T(8,128)S(1)} %bitcast.5) | data formatting | bytes 2097152
  (1 shorter events, 0.0 us)
Async XLA Ops:
  0.6 0.7 copy-start.4
  0.6 0.7 copy-start.5
  1.3 0.9 %copy-start = (bf16[256,512]{1,0:T(8,128)(2,1)S(1)}, bf16[256,512]{1,0:T(8,128)(2,1)}, u32[]{:S(2)}) copy-start(bf16[256,512]{1,0:T(8,128)(2,1)} %param.7) | copy-start | bytes 786436
  2.3 1.0 %copy-start.1 = (bf16[512,512]{1,0:T(8,128)(2,1)S(1)}, bf16[512,512]{1,0:T(8,128)(2,1)}, u32[]{:S(2)}) copy-start(bf16[512,512]{1,0:T(8,128)(2,1)} %param.6) | copy-start | bytes 1572868
  3.3 0.9 %copy-start.2 = (bf16[8,128,128]{2,1,0:T(8,128)(2,1)S(1)}, bf16[8,128,128]{2,1,0:T(8,128)(2,1)}, u32[]{:S(2)}) copy-start(bf16[8,128,128]{2,1,0:T(8,128)(2,1)} %w_hbm.1) | copy-start | bytes 786436
  4.2 0.9 %copy-start.3 = (bf16[8,128,128]{2,1,0:T(8,128)(2,1)S(1)}, bf16[8,128,128]{2,1,0:T(8,128)(2,1)}, u32[]{:S(2)}) copy-start(bf16[8,128,128]{2,1,0:T(8,128)(2,1)} %t_hbm.1) | copy-start | bytes 786436

commit v2 on v1

v2 whole, which is shorter than its diff:
```python
import jax
import jax.numpy as jnp
from jax import lax
from jax.experimental import pallas as pl
from jax.experimental.pallas import tpu as pltpu
from jax.sharding import PartitionSpec as P

MESH = pl.DeviceIdType.MESH
NX, NY = 4, 8
STEPS = [0, -1, 1, -2, 2, -3, 3, 4]
GROUPS = [[0], [1, 2], [3, 4], [5, 6], [7]]
VMEM = 56 << 20
FULL_BARRIER = 0
F32 = jnp.float32
BF16 = jnp.bfloat16


def dot(a, b, ca, cb):
    return lax.dot_general(a, b, (((ca,), (cb,)), ((), ())), preferred_element_type=F32)


def kernel(
    obs_user, obs_item, u_hbm, v_hbm, w_hbm, t_hbm, ug_hbm, ig_hbm,
    uv, vt, wv, tv, ta, tb, xa, xb, ys, yr, qa, qb, za, zb, z1, tr, ob, rm, gh, ug, ig,
    sem_in, sem_out, ag_s, ag_r, sb_s, sb_r, xa_s, xa_r, xb_s, xb_r,
    y_s, y_r, z_s, z_r, g_s, g_r,
):
    r = lax.axis_index("rows")
    y = lax.axis_index("grp")
    c = lax.rem(r, 2)
    x = lax.rem(r // 2, NX)
    z = r // (2 * NX)
    i, g = lax.rem(z, 4), z // 4

    def dev(dx=0, dy=0, di=0, dg=0, dc=0):
        cc = 1 - c if dc else c
        xx = lax.rem(x + dx, NX) if dx else x
        yy = lax.rem(y + dy + NY, NY) if dy else y
        gg = lax.rem(g + dg, 3) if dg else g
        zz = gg * 4 + (lax.rem(i + di, 4) if di else i)
        return ((zz * NX + xx) * 2 + cc, yy)

    def yat(d):
        return lax.rem(y + STEPS[d] + NY, NY)

    def remote(src, dst, s, t, to):
        return pltpu.make_async_remote_copy(src, dst, s, t, device_id=to, device_id_type=MESH)

    pending = []
    outs = []

    def send(cp):
        cp.start()
        pending.append(cp)

    loads = [
        pltpu.make_async_copy(v_hbm, vt.at[pl.ds(2 * y, 2)], sem_in.at[0]),
        pltpu.make_async_copy(u_hbm, uv, sem_in.at[1]),
        pltpu.make_async_copy(w_hbm, wv, sem_in.at[2]),
        pltpu.make_async_copy(t_hbm, tv, sem_in.at[3]),
    ]
    for cp in loads:
        cp.start()

    peers = [dev(dy=1), dev(dy=-1), dev(dc=1)]
    peers += [dev(dx=d, dc=dc) for d in range(1, 4) for dc in range(2)]
    peers += [dev(di=d, dc=dc) for d in range(1, 4) for dc in range(2)]
    peers += [dev(dg=1), dev(dg=2)]
    if FULL_BARRIER:
        peers += [dev(dy=d) for d in range(2, 7)]
        peers += [dev(dx=dx, di=di) for dx in range(1, 4) for di in range(1, 4)]
    barrier = pltpu.get_barrier_semaphore()
    for p in peers:
        pl.semaphore_signal(barrier, inc=1, device_id=p, device_id_type=MESH)
    for cp in loads:
        cp.wait()
    pl.semaphore_wait(barrier, len(peers))

    def ag(direction, step, h):
        sgn = 1 if direction == 0 else -1
        src_y = lax.rem(y - sgn * (step - 1) + NY, NY)
        ref = vt.at[2 * src_y + c, h]
        k = (direction * 4 + step - 1) * 2 + h
        return remote(ref, ref, ag_s.at[k], ag_r.at[k], dev(dy=sgn))

    def ag_has(direction, step, h):
        return step < 4 or h == direction

    def to_sibling(d, h):
        ref = vt.at[2 * yat(d) + c, h]
        return remote(ref, ref, sb_s.at[2 * d + h], sb_r.at[2 * d + h], dev(dc=1))

    def tile(d, dc):
        yy = yat(d)
        cc = 1 - c if dc else c
        b = 2 * yy + cc
        k = jnp.int32(0)
        scale = F32(0.0)
        for n in range(8):
            hit = obs_item[n] == b
            k = jnp.where(hit, n, k)
            scale = jnp.where(hit, F32(0.0625), scale)
        j = obs_user[k]
        uk = uv[j]
        vb = vt[b].reshape(128, 512)
        predicted = dot(uk, vb, 1, 1)
        res = (wv[k].astype(F32) * (predicted - tv[k].astype(F32)) * scale).astype(BF16)
        term = dot(res, uk, 0, 0)
        for n in range(4):
            ta[d, dc, n] = term[24 * n : 24 * n + 24].astype(BF16)
            tb[d, dc, n] = term[96 + 8 * n : 104 + 8 * n].astype(BF16)
        for jj in range(4):
            keep = jnp.where(j == jj, F32(1.0), F32(0.0)).astype(BF16)
            rm[b, jj] = res * keep

    def terms(grp, dc):
        ds = GROUPS[grp]
        dd = pl.ds(ds[0], len(ds))
        for n in range(NX):
            if n or dc:
                e = n * 2 + dc
                k = grp * 8 + e
                xx = lax.rem(x + n, NX)
                ii = lax.rem(i + n, 4)
                send(remote(ta.at[dd, dc, xx], xa.at[dd, e], xa_s.at[k], xa_r.at[k], dev(dx=n, dc=dc)))
                send(remote(tb.at[dd, dc, ii], xb.at[dd, e], xb_s.at[k], xb_r.at[k], dev(di=n, dc=dc)))

    def reduce_group(grp):
        ds = GROUPS[grp]
        dd = pl.ds(ds[0], len(ds))
        for e in range(1, 8):
            k = grp * 8 + e
            remote(xa.at[dd, e], xa.at[dd, e], xa_s.at[k], xa_r.at[k], dev(dc=1)).wait_recv()
            remote(xb.at[dd, e], xb.at[dd, e], xb_s.at[k], xb_r.at[k], dev(dc=1)).wait_recv()
        for d in ds:
            sa = ta[d, 0, x].astype(F32)
            sb = tb[d, 0, i].astype(F32)
            for e in range(1, 8):
                sa = sa + xa[d, e].astype(F32)
                sb = sb + xb[d, e].astype(F32)
            dst = ys if d else yr
            dst[d, 0:24] = sa
            dst[d, 24:32] = sb
            if d:
                send(remote(ys.at[d], yr.at[d], y_s.at[d], y_r.at[d], dev(dy=STEPS[d])))

    def arrive(step, h):
        for direction in range(2):
            if ag_has(direction, step, h):
                ag(direction, step, h).wait_recv()
                if step < 4 and ag_has(direction, step + 1, h):
                    send(ag(direction, step + 1, h))
                send(to_sibling(GROUPS[step][direction] if step < 4 else 7, h))

    def other(d):
        for h in range(2):
            to_sibling(d, h).wait_recv()
        tile(d, 1)

    for h in range(2):
        for direction in range(2):
            send(ag(direction, 1, h))
    tile(0, 1)
    terms(0, 1)
    tile(0, 0)
    terms(0, 0)
    arrive(1, 0)
    arrive(1, 1)
    for step in range(1, 4):
        low, high = GROUPS[step]
        tile(low, 0)
        arrive(step + 1, 0)
        tile(high, 0)
        terms(step, 0)
        arrive(step + 1, 1)
        other(low)
        other(high)
        terms(step, 1)
        reduce_group(step - 1)
    tile(7, 0)
    terms(4, 0)
    other(7)
    terms(4, 1)
    reduce_group(3)
    reduce_group(4)

    table = vt[...].reshape(2048, 512)
    gram = 0.05 * dot(table, table, 0, 0)
    hi = gram.astype(BF16)
    gh[0] = hi
    rest = gram - hi.astype(F32)
    mid = rest.astype(BF16)
    gh[1] = mid
    gh[2] = (rest - mid.astype(F32)).astype(BF16)

    total = yr[0]
    for d in range(1, 8):
        remote(yr.at[d], yr.at[d], y_s.at[d], y_r.at[d], dev(dc=1)).wait_recv()
        total = total + yr[d]
    for n in range(4):
        qa[n] = total[0:24, 128 * n : 128 * n + 128]
        qb[n] = total[24:32, 128 * n : 128 * n + 128]
    for d in range(1, 4):
        send(remote(qa.at[lax.rem(i + d, 4)], za.at[d], z_s.at[d], z_r.at[d], dev(di=d)))
        send(remote(qb.at[lax.rem(x + d, 4)], zb.at[d], z_s.at[4 + d], z_r.at[4 + d], dev(dx=d)))

    def user(j):
        uj = uv[j]
        acc = 0.1 * uj.astype(F32)
        for n in range(3):
            acc = acc + dot(uj, gh[n], 1, 0)
        for b in range(16):
            acc = acc + dot(rm[b, j], vt[b].reshape(128, 512), 1, 0)
        ug[j] = acc
        cp = pltpu.make_async_copy(ug.at[j], ug_hbm.at[j], sem_out.at[j])
        cp.start()
        outs.append(cp)

    user(0)
    user(1)

    pa, pb = qa[i], qb[x]
    for d in range(1, 4):
        remote(za.at[d], za.at[d], z_s.at[d], z_r.at[d], dev(dc=1)).wait_recv()
        remote(zb.at[d], zb.at[d], z_s.at[4 + d], z_r.at[4 + d], dev(dc=1)).wait_recv()
        pa = pa + za[d]
        pb = pb + zb[d]
    z1[0:24] = pa
    z1[24:32] = pb
    for d in range(1, 3):
        send(remote(z1, tr.at[g], z_s.at[8 + d], z_r.at[8 + d], dev(dg=d)))
    tr[g] = z1[...]
    user(2)
    user(3)
    for d in range(1, 3):
        remote(z1, z1, z_s.at[8 + d], z_r.at[8 + d], dev(dc=1)).wait_recv()
    ob[c, x, i] = tr[0] + tr[1] + tr[2]

    def spread(ref, k, to):
        return remote(ref, ref, g_s.at[k], g_r.at[k], to)

    for dx in range(NX):
        for di in range(4):
            if dx or di:
                send(spread(ob.at[c, x, i], dx * 4 + di, dev(dx=dx, di=di)))
    for dx in range(NX):
        for di in range(4):
            if dx or di:
                spread(ob.at[c, x, i], dx * 4 + di, dev(dx=dx, di=di)).wait_recv()
        send(spread(ob.at[c, lax.rem(x + NX - dx, NX)], 16 + dx, dev(dc=1)))
    for dx in range(NX):
        spread(ob.at[c, x], 16 + dx, dev(dc=1)).wait_recv()
    own = vt[pl.ds(2 * y, 2)].reshape(256, 512)
    for cc in range(2):
        for xx in range(NX):
            for ii in range(4):
                lo = cc * 128 + 24 * xx
                ig[lo : lo + 24, 128 * ii : 128 * ii + 128] = ob[cc, xx, ii, 0:24]
                lo = cc * 128 + 96 + 8 * ii
                ig[lo : lo + 8, 128 * xx : 128 * xx + 128] = ob[cc, xx, ii, 24:32]
    ig[...] = ig[...] * (1.0 / 32.0) + 0.1 * own.astype(F32)
    cp = pltpu.make_async_copy(ig, ig_hbm, sem_out.at[4])
    cp.start()
    outs.append(cp)
    for cp in pending:
        cp.wait_send()
    for cp in outs:
        cp.wait()


def place(ug, ig, ug_out, ig_out, uv, iv, sem):
    parts = [(ug.at[j], uv.at[j], ug_out.at[j]) for j in range(4)] + [(ig, iv, ig_out)]
    fetch = [pltpu.make_async_copy(p[0], p[1], sem.at[0, n]) for n, p in enumerate(parts)]
    store = [pltpu.make_async_copy(p[1], p[2], sem.at[1, n]) for n, p in enumerate(parts)]
    for cp in fetch:
        cp.start()
    for f, t in zip(fetch, store):
        f.wait()
        t.start()
    for cp in store:
        cp.wait()


def local(user_factors, item_factors, obs_user, obs_item, obs_weight, obs_target):
    hbm = pl.BlockSpec(memory_space=pltpu.HBM)
    smem = pl.BlockSpec(memory_space=pltpu.SMEM)
    dma = pltpu.SemaphoreType.DMA
    shapes = (
        jax.ShapeDtypeStruct((4, 128, 512), F32),
        jax.ShapeDtypeStruct((256, 512), F32),
    )
    made = pl.pallas_call(
        kernel,
        out_shape=shapes,
        in_specs=[smem, smem, hbm, hbm, hbm, hbm],
        out_specs=(hbm, hbm),
        scratch_shapes=[
            pltpu.VMEM((4, 128, 512), BF16),
            pltpu.VMEM((16, 2, 64, 512), BF16),
            pltpu.VMEM((8, 128, 128), BF16),
            pltpu.VMEM((8, 128, 128), BF16),
            pltpu.VMEM((8, 2, 4, 24, 512), BF16),
            pltpu.VMEM((8, 2, 4, 8, 512), BF16),
            pltpu.VMEM((8, 8, 24, 512), BF16),
            pltpu.VMEM((8, 8, 8, 512), BF16),
            pltpu.VMEM((8, 32, 512), F32),
            pltpu.VMEM((8, 32, 512), F32),
            pltpu.VMEM((4, 24, 128), F32),
            pltpu.VMEM((4, 8, 128), F32),
            pltpu.VMEM((4, 24, 128), F32),
            pltpu.VMEM((4, 8, 128), F32),
            pltpu.VMEM((32, 128), F32),
            pltpu.VMEM((3, 32, 128), F32),
            pltpu.VMEM((2, 4, 4, 32, 128), F32),
            pltpu.VMEM((16, 4, 128, 128), BF16),
            pltpu.VMEM((3, 512, 512), BF16),
            pltpu.VMEM((4, 128, 512), F32),
            pltpu.VMEM((256, 512), F32),
            dma((4,)), dma((5,)),
            dma((16,)), dma((16,)),
            dma((16,)), dma((16,)),
            dma((40,)), dma((40,)),
            dma((40,)), dma((40,)),
            dma((8,)), dma((8,)),
            dma((12,)), dma((12,)),
            dma((20,)), dma((20,)),
        ],
        compiler_params=pltpu.CompilerParams(
            collective_id=0, has_side_effects=True, vmem_limit_bytes=VMEM
        ),
    )(
        obs_user,
        obs_item,
        user_factors.reshape(4, 128, 512),
        item_factors.reshape(2, 2, 64, 512),
        obs_weight,
        obs_target,
    )
    user_grad, item_grad = pl.pallas_call(
        place,
        out_shape=shapes,
        in_specs=[hbm, hbm],
        out_specs=(hbm, hbm),
        scratch_shapes=[pltpu.VMEM((4, 128, 512), F32), pltpu.VMEM((256, 512), F32), dma((2, 5))],
        compiler_params=pltpu.CompilerParams(vmem_limit_bytes=VMEM),
    )(*made)
    return user_grad.reshape(512, 512), item_grad


def solution(mesh):
    both = P(("rows", "grp"))
    placed = (
        P(("rows", "grp"), None),
        P("grp", None),
        both,
        both,
        P(("rows", "grp"), None, None),
        P(("rows", "grp"), None, None),
    )
    return jax.shard_map(
        local,
        mesh=mesh,
        in_specs=placed,
        out_specs=(P(("rows", "grp"), None), P("grp", None)),
        check_vma=False,
    )
```

time: 82.1 us -> 76.1 us (0.927)
  local copies, waits for them, and re-layouts: 5.51 us -> 0 us
  other arithmetic: 0.91 us -> 0 us
    unnamed x13 -> x0, local copies, waits for them, and re-layouts: 5.51 us -> none
    add x1 -> x0, other arithmetic: 0.87 us -> none  [local(): item_sum.reshape(256, 512) / 32.0 + 0.1 * item_factors.astype(F32)]
    pallas_call x1 -> x2, Pallas kernels: 74.7 us -> 75.2 us  [the longest x1 73 us: local(): pl.pallas_call(kernel, out_shape=shapes, in_specs=[smem, smem, hbm, hbm,...]
where the time goes in v2:
time: 76.1 us; the launch traced here: 75.9 us
  Pallas kernels  75.2 us (99%)
    pallas_call x1, Pallas kernels, local(): pl.pallas_call(kernel, out_shape=shapes, in_specs=[smem, smem, hbm, hbm,...  73 us
    pallas_call x1, Pallas kernels, local(): pl.pallas_call(place, out_shape=shapes, in_specs=[hbm, hbm], out_specs=(h...  2.24 us

profile of v2, /device:TPU:1, one launch (start us, length us, event | category | flops | bytes accessed | tf_op | source)
XLA Modules:
  0.0 75.9 jit_solution(16327403376663202049)
XLA Ops:
  0.6 73.0 %shard_map.77 = (f32[4,128,512]{2,1,0:T(8,128)}, f32[256,512]{1,0:T(8,128)}) custom-call(s32[8]{0:T(128)} %obs_user.1, s32[8]{0:T(128)} %obs_item.1, bf16[4,128,512]{2,1,0:T(8,128)(2,1)} %bitcast.3, bf16[2,2,64,512]{3,2,1,0:T(8,128)(2,1)} %bitcast.4, bf16[8,128,128]{2,1,0:T(8,128)(2,1)} %w_hbm.1, bf16[8,128,128]{2,1,0:T(8,128)(2,1)} %t_hbm.1), custom_call_target="tpu_custom_call" | custom-call | tf_op jit(solution)/shard_map/pallas_call | solution.py:292
  73.6 2.2 %shard_map.78 = (f32[4,128,512]{2,1,0:T(8,128)}, f32[256,512]{1,0:T(8,128)}) custom-call(f32[4,128,512]{2,1,0:T(8,128)} %get-tuple-element.6.ug, f32[256,512]{1,0:T(8,128)} %get-tuple-element.7.ig), custom_call_target="tpu_custom_call" | custom-call | tf_op jit(solution)/shard_map/pallas_call | solution.py:339

commit v3 on v2

--- a/solution.py
+++ b/solution.py
@@ -20,9 +20,9 @@
 
 
 def kernel(
-    obs_user, obs_item, u_hbm, v_hbm, w_hbm, t_hbm, ug_hbm, ig_hbm,
-    uv, vt, wv, tv, ta, tb, xa, xb, ys, yr, qa, qb, za, zb, z1, tr, ob, rm, gh, ug, ig,
-    sem_in, sem_out, ag_s, ag_r, sb_s, sb_r, xa_s, xa_r, xb_s, xb_r,
+    obs_user, obs_item, u_hbm, v_hbm, w_hbm, t_hbm, ug, ig,
+    uv, vt, wv, tv, ta, tb, xa, xb, ys, yr, qa, qb, za, zb, z1, tr, ob, rm, gh,
+    sem_in, ag_s, ag_r, sb_s, sb_r, xa_s, xa_r, xb_s, xb_r,
     y_s, y_r, z_s, z_r, g_s, g_r,
 ):
     r = lax.axis_index("rows")
@@ -47,7 +47,10 @@
         return pltpu.make_async_remote_copy(src, dst, s, t, device_id=to, device_id_type=MESH)
 
     pending = []
-    outs = []
+
+    def drain(keep=0):
+        while len(pending) > keep:
+            pending.pop(0).wait_send()
 
     def send(cp):
         cp.start()
@@ -116,7 +119,7 @@
     def terms(grp, dc):
         ds = GROUPS[grp]
         dd = pl.ds(ds[0], len(ds))
-        for n in range(NX):
+        for n in (2, 1, 3, 0):
             if n or dc:
                 e = n * 2 + dc
                 k = grp * 8 + e
@@ -145,22 +148,24 @@
                 send(remote(ys.at[d], yr.at[d], y_s.at[d], y_r.at[d], dev(dy=STEPS[d])))
 
     def arrive(step, h):
-        for direction in range(2):
-            if ag_has(direction, step, h):
-                ag(direction, step, h).wait_recv()
-                if step < 4 and ag_has(direction, step + 1, h):
-                    send(ag(direction, step + 1, h))
-                send(to_sibling(GROUPS[step][direction] if step < 4 else 7, h))
+        came = [direction for direction in range(2) if ag_has(direction, step, h)]
+        for direction in came:
+            ag(direction, step, h).wait_recv()
+            if step < 4 and ag_has(direction, step + 1, h):
+                send(ag(direction, step + 1, h))
+        for direction in came:
+            send(to_sibling(GROUPS[step][direction] if step < 4 else 7, h))
 
     def other(d):
         for h in range(2):
             to_sibling(d, h).wait_recv()
         tile(d, 1)
 
-    for h in range(2):
-        for direction in range(2):
-            send(ag(direction, 1, h))
+    for direction in range(2):
+        send(ag(direction, 1, 0))
     tile(0, 1)
+    for direction in range(2):
+        send(ag(direction, 1, 1))
     terms(0, 1)
     tile(0, 0)
     terms(0, 0)
@@ -193,6 +198,7 @@
     gh[1] = mid
     gh[2] = (rest - mid.astype(F32)).astype(BF16)
 
+    drain(7)
     total = yr[0]
     for d in range(1, 8):
         remote(yr.at[d], yr.at[d], y_s.at[d], y_r.at[d], dev(dc=1)).wait_recv()
@@ -212,9 +218,6 @@
         for b in range(16):
             acc = acc + dot(rm[b, j], vt[b].reshape(128, 512), 1, 0)
         ug[j] = acc
-        cp = pltpu.make_async_copy(ug.at[j], ug_hbm.at[j], sem_out.at[j])
-        cp.start()
-        outs.append(cp)
 
     user(0)
     user(1)
@@ -232,6 +235,7 @@
     tr[g] = z1[...]
     user(2)
     user(3)
+    drain(2)
     for d in range(1, 3):
         remote(z1, z1, z_s.at[8 + d], z_r.at[8 + d], dev(dc=1)).wait_recv()
     ob[c, x, i] = tr[0] + tr[1] + tr[2]
@@ -239,15 +243,16 @@
     def spread(ref, k, to):
         return remote(ref, ref, g_s.at[k], g_r.at[k], to)
 
-    for dx in range(NX):
-        for di in range(4):
+    for dx in (2, 1, 3, 0):
+        for di in (2, 1, 3, 0):
             if dx or di:
                 send(spread(ob.at[c, x, i], dx * 4 + di, dev(dx=dx, di=di)))
-    for dx in range(NX):
+    for dx in (0, 1, 3, 2):
         for di in range(4):
             if dx or di:
                 spread(ob.at[c, x, i], dx * 4 + di, dev(dx=dx, di=di)).wait_recv()
         send(spread(ob.at[c, lax.rem(x + NX - dx, NX)], 16 + dx, dev(dc=1)))
+    drain()
     for dx in range(NX):
         spread(ob.at[c, x], 16 + dx, dev(dc=1)).wait_recv()
     own = vt[pl.ds(2 * y, 2)].reshape(256, 512)
@@ -259,30 +264,20 @@
                 lo = cc * 128 + 96 + 8 * ii
                 ig[lo : lo + 8, 128 * xx : 128 * xx + 128] = ob[cc, xx, ii, 24:32]
     ig[...] = ig[...] * (1.0 / 32.0) + 0.1 * own.astype(F32)
-    cp = pltpu.make_async_copy(ig, ig_hbm, sem_out.at[4])
-    cp.start()
-    outs.append(cp)
-    for cp in pending:
-        cp.wait_send()
-    for cp in outs:
-        cp.wait()
-
-
-def place(ug, ig, ug_out, ig_out, uv, iv, sem):
-    parts = [(ug.at[j], uv.at[j], ug_out.at[j]) for j in range(4)] + [(ig, iv, ig_out)]
-    fetch = [pltpu.make_async_copy(p[0], p[1], sem.at[0, n]) for n, p in enumerate(parts)]
-    store = [pltpu.make_async_copy(p[1], p[2], sem.at[1, n]) for n, p in enumerate(parts)]
-    for cp in fetch:
+
+
+def place(ug, ig, ug_out, ig_out, sem):
+    cps = [pltpu.make_async_copy(ug.at[j], ug_out.at[j], sem.at[j]) for j in range(4)]
+    cps.append(pltpu.make_async_copy(ig, ig_out, sem.at[4]))
+    for cp in cps:
         cp.start()
-    for f, t in zip(fetch, store):
-        f.wait()
-        t.start()
-    for cp in store:
+    for cp in cps:
         cp.wait()
 
 
 def local(user_factors, item_factors, obs_user, obs_item, obs_weight, obs_target):
     hbm = pl.BlockSpec(memory_space=pltpu.HBM)
+    vmem = pl.BlockSpec(memory_space=pltpu.VMEM)
     smem = pl.BlockSpec(memory_space=pltpu.SMEM)
     dma = pltpu.SemaphoreType.DMA
     shapes = (
@@ -291,9 +286,9 @@
     )
     made = pl.pallas_call(
         kernel,
-        out_shape=shapes,
+        out_shape=tuple(pltpu.VMEM(a.shape, a.dtype) for a in shapes),
         in_specs=[smem, smem, hbm, hbm, hbm, hbm],
-        out_specs=(hbm, hbm),
+        out_specs=(vmem, vmem),
         scratch_shapes=[
             pltpu.VMEM((4, 128, 512), BF16),
             pltpu.VMEM((16, 2, 64, 512), BF16),
@@ -314,9 +309,7 @@
             pltpu.VMEM((2, 4, 4, 32, 128), F32),
             pltpu.VMEM((16, 4, 128, 128), BF16),
             pltpu.VMEM((3, 512, 512), BF16),
-            pltpu.VMEM((4, 128, 512), F32),
-            pltpu.VMEM((256, 512), F32),
-            dma((4,)), dma((5,)),
+            dma((4,)),
             dma((16,)), dma((16,)),
             dma((16,)), dma((16,)),
             dma((40,)), dma((40,)),
@@ -339,11 +332,11 @@
     user_grad, item_grad = pl.pallas_call(
         place,
         out_shape=shapes,
-        in_specs=[hbm, hbm],
+        in_specs=[vmem, vmem],
         out_specs=(hbm, hbm),
-        scratch_shapes=[pltpu.VMEM((4, 128, 512), F32), pltpu.VMEM((256, 512), F32), dma((2, 5))],
+        scratch_shapes=[dma((5,))],
         compiler_params=pltpu.CompilerParams(vmem_limit_bytes=VMEM),
-    )(*made)
+    )(*(pltpu.with_memory_space_constraint(m, pltpu.VMEM) for m in made))
     return user_grad.reshape(512, 512), item_grad
 
 

time: 76.1 us -> 73.3 us (0.963)
  Pallas kernels: 75.2 us -> 72.5 us
    pallas_call x2, Pallas kernels: 75.2 us -> 72.5 us  [the longest x1 71.3 us: local(): pl.pallas_call(kernel, out_shape=tuple((pltpu.VMEM(a.shape, a.dtype) for...]
where the time goes in v3:
time: 73.3 us; the launch traced here: 73.1 us
  Pallas kernels  72.5 us (99%)
    pallas_call x1, Pallas kernels, local(): pl.pallas_call(kernel, out_shape=tuple((pltpu.VMEM(a.shape, a.dtype) for...  71.3 us

profile of v3, /device:TPU:1, one launch (start us, length us, event | category | flops | bytes accessed | tf_op | source)
XLA Modules:
  0.0 73.1 jit_solution(15140659562050388082)
XLA Ops:
  0.6 71.3 %shard_map.77 = (f32[4,128,512]{2,1,0:T(8,128)S(1)}, f32[256,512]{1,0:T(8,128)S(1)}) custom-call(s32[8]{0:T(128)} %obs_user.1, s32[8]{0:T(128)} %obs_item.1, bf16[4,128,512]{2,1,0:T(8,128)(2,1)} %bitcast.3, bf16[2,2,64,512]{3,2,1,0:T(8,128)(2,1)} %bitcast.4, bf16[8,128,128]{2,1,0:T(8,128)(2,1)} %w_hbm.1, bf16[8,128,128]{2,1,0:T(8,128)(2,1)} %t_hbm.1), custom_call_target="tpu_custom_call" | custom-call | tf_op jit(solution)/shard_map/pallas_call | solution.py:287
  72.0 1.2 %shard_map.78 = (f32[4,128,512]{2,1,0:T(8,128)}, f32[256,512]{1,0:T(8,128)}) custom-call(f32[4,128,512]{2,1,0:T(8,128)S(1)} %get-tuple-element.6.ug, f32[256,512]{1,0:T(8,128)S(1)} %get-tuple-element.7.ig), custom_call_target="tpu_custom_call" | custom-call | tf_op jit(solution)/shard_map/pallas_call | solution.py:332

commit v4 on v3

--- a/solution.py
+++ b/solution.py
@@ -20,8 +20,8 @@
 
 
 def kernel(
-    obs_user, obs_item, u_hbm, v_hbm, w_hbm, t_hbm, ug, ig,
-    uv, vt, wv, tv, ta, tb, xa, xb, ys, yr, qa, qb, za, zb, z1, tr, ob, rm, gh,
+    user_hbm, item_hbm, u_hbm, v_hbm, w_hbm, t_hbm, ug, ig,
+    obs_user, obs_item, uv, vt, wv, tv, ta, tb, xa, xb, ys, yr, qa, qb, za, zb, z1, tr, ob, rm, gh,
     sem_in, ag_s, ag_r, sb_s, sb_r, xa_s, xa_r, xb_s, xb_r,
     y_s, y_r, z_s, z_r, g_s, g_r,
 ):
@@ -56,15 +56,6 @@
         cp.start()
         pending.append(cp)
 
-    loads = [
-        pltpu.make_async_copy(v_hbm, vt.at[pl.ds(2 * y, 2)], sem_in.at[0]),
-        pltpu.make_async_copy(u_hbm, uv, sem_in.at[1]),
-        pltpu.make_async_copy(w_hbm, wv, sem_in.at[2]),
-        pltpu.make_async_copy(t_hbm, tv, sem_in.at[3]),
-    ]
-    for cp in loads:
-        cp.start()
-
     peers = [dev(dy=1), dev(dy=-1), dev(dc=1)]
     peers += [dev(dx=d, dc=dc) for d in range(1, 4) for dc in range(2)]
     peers += [dev(di=d, dc=dc) for d in range(1, 4) for dc in range(2)]
@@ -73,8 +64,18 @@
         peers += [dev(dy=d) for d in range(2, 7)]
         peers += [dev(dx=dx, di=di) for dx in range(1, 4) for di in range(1, 4)]
     barrier = pltpu.get_barrier_semaphore()
-    for p in peers:
+    for p in reversed(peers):
         pl.semaphore_signal(barrier, inc=1, device_id=p, device_id_type=MESH)
+    loads = [
+        pltpu.make_async_copy(v_hbm, vt.at[pl.ds(2 * y, 2)], sem_in.at[0]),
+        pltpu.make_async_copy(u_hbm, uv, sem_in.at[1]),
+        pltpu.make_async_copy(w_hbm, wv, sem_in.at[2]),
+        pltpu.make_async_copy(t_hbm, tv, sem_in.at[3]),
+        pltpu.make_async_copy(user_hbm, obs_user, sem_in.at[4]),
+        pltpu.make_async_copy(item_hbm, obs_item, sem_in.at[5]),
+    ]
+    for cp in loads:
+        cp.start()
     for cp in loads:
         cp.wait()
     pl.semaphore_wait(barrier, len(peers))
@@ -161,11 +162,10 @@
             to_sibling(d, h).wait_recv()
         tile(d, 1)
 
-    for direction in range(2):
-        send(ag(direction, 1, 0))
+    for h in range(2):
+        for direction in range(2):
+            send(ag(direction, 1, h))
     tile(0, 1)
-    for direction in range(2):
-        send(ag(direction, 1, 1))
     terms(0, 1)
     tile(0, 0)
     terms(0, 0)
@@ -278,7 +278,6 @@
 def local(user_factors, item_factors, obs_user, obs_item, obs_weight, obs_target):
     hbm = pl.BlockSpec(memory_space=pltpu.HBM)
     vmem = pl.BlockSpec(memory_space=pltpu.VMEM)
-    smem = pl.BlockSpec(memory_space=pltpu.SMEM)
     dma = pltpu.SemaphoreType.DMA
     shapes = (
         jax.ShapeDtypeStruct((4, 128, 512), F32),
@@ -287,9 +286,11 @@
     made = pl.pallas_call(
         kernel,
         out_shape=tuple(pltpu.VMEM(a.shape, a.dtype) for a in shapes),
-        in_specs=[smem, smem, hbm, hbm, hbm, hbm],
+        in_specs=[hbm, hbm, hbm, hbm, hbm, hbm],
         out_specs=(vmem, vmem),
         scratch_shapes=[
+            pltpu.SMEM((8,), jnp.int32),
+            pltpu.SMEM((8,), jnp.int32),
             pltpu.VMEM((4, 128, 512), BF16),
             pltpu.VMEM((16, 2, 64, 512), BF16),
             pltpu.VMEM((8, 128, 128), BF16),
@@ -309,7 +310,7 @@
             pltpu.VMEM((2, 4, 4, 32, 128), F32),
             pltpu.VMEM((16, 4, 128, 128), BF16),
             pltpu.VMEM((3, 512, 512), BF16),
-            dma((4,)),
+            dma((6,)),
             dma((16,)), dma((16,)),
             dma((16,)), dma((16,)),
             dma((40,)), dma((40,)),

time: 73.3 us -> 72 us (0.982)
  Pallas kernels: 72.5 us -> 71.2 us
    pallas_call x1, Pallas kernels: 71.3 us -> 70.1 us  [local(): pl.pallas_call(kernel, out_shape=tuple((pltpu.VMEM(a.shape, a.dtype) for...]
where the time goes in v4:
time: 72 us; the launch traced here: 71.9 us
  Pallas kernels  71.2 us (99%)
    pallas_call x1, Pallas kernels, local(): pl.pallas_call(kernel, out_shape=tuple((pltpu.VMEM(a.shape, a.dtype) for...  70.1 us

profile of v4, /device:TPU:1, one launch (start us, length us, event | category | flops | bytes accessed | tf_op | source)
XLA Modules:
  0.0 71.9 jit_solution(8064983283907711746)
XLA Ops:
  0.6 70.1 %shard_map.77 = (f32[4,128,512]{2,1,0:T(8,128)S(1)}, f32[256,512]{1,0:T(8,128)S(1)}) custom-call(s32[8]{0:T(128)} %user_hbm.1, s32[8]{0:T(128)} %item_hbm.1, bf16[4,128,512]{2,1,0:T(8,128)(2,1)} %bitcast.3, bf16[2,2,64,512]{3,2,1,0:T(8,128)(2,1)} %bitcast.4, bf16[8,128,128]{2,1,0:T(8,128)(2,1)} %w_hbm.1, bf16[8,128,128]{2,1,0:T(8,128)(2,1)} %t_hbm.1), custom_call_target="tpu_custom_call" | custom-call | tf_op jit(solution)/shard_map/pallas_call | solution.py:286
  70.7 1.2 %shard_map.78 = (f32[4,128,512]{2,1,0:T(8,128)}, f32[256,512]{1,0:T(8,128)}) custom-call(f32[4,128,512]{2,1,0:T(8,128)S(1)} %get-tuple-element.6.ug, f32[256,512]{1,0:T(8,128)S(1)} %get-tuple-element.7.ig), custom_call_target="tpu_custom_call" | custom-call | tf_op jit(solution)/shard_map/pallas_call | solution.py:333

commit v5 on v4

--- a/solution.py
+++ b/solution.py
@@ -247,23 +247,30 @@
         for di in (2, 1, 3, 0):
             if dx or di:
                 send(spread(ob.at[c, x, i], dx * 4 + di, dev(dx=dx, di=di)))
+    own = vt[pl.ds(2 * y, 2)].reshape(256, 512)
+    ig[...] = 0.1 * own.astype(F32)
     for dx in (0, 1, 3, 2):
         for di in range(4):
             if dx or di:
                 spread(ob.at[c, x, i], dx * 4 + di, dev(dx=dx, di=di)).wait_recv()
         send(spread(ob.at[c, lax.rem(x + NX - dx, NX)], 16 + dx, dev(dc=1)))
+    half = pl.multiple_of(c * 128, 128)
+
+    def settle(cc, start):
+        for xx in range(NX):
+            for ii in range(4):
+                cols = slice(128 * ii, 128 * ii + 128)
+                rows = pl.ds(pl.multiple_of(start + 24 * xx, 8), 24)
+                ig[rows, cols] = ig[rows, cols] + ob[cc, xx, ii, 0:24] * (1.0 / 32.0)
+                cols = slice(128 * xx, 128 * xx + 128)
+                rows = pl.ds(pl.multiple_of(start + 96 + 8 * ii, 8), 8)
+                ig[rows, cols] = ig[rows, cols] + ob[cc, xx, ii, 24:32] * (1.0 / 32.0)
+
+    settle(c, half)
     drain()
     for dx in range(NX):
         spread(ob.at[c, x], 16 + dx, dev(dc=1)).wait_recv()
-    own = vt[pl.ds(2 * y, 2)].reshape(256, 512)
-    for cc in range(2):
-        for xx in range(NX):
-            for ii in range(4):
-                lo = cc * 128 + 24 * xx
-                ig[lo : lo + 24, 128 * ii : 128 * ii + 128] = ob[cc, xx, ii, 0:24]
-                lo = cc * 128 + 96 + 8 * ii
-                ig[lo : lo + 8, 128 * xx : 128 * xx + 128] = ob[cc, xx, ii, 24:32]
-    ig[...] = ig[...] * (1.0 / 32.0) + 0.1 * own.astype(F32)
+    settle(1 - c, pl.multiple_of(128 - c * 128, 128))
 
 
 def place(ug, ig, ug_out, ig_out, sem):

time: 72 us -> 72 us (level)
  no operation moved by 1% of the time
where the time goes in v5:
time: 72 us; the launch traced here: 71.8 us
  Pallas kernels  71.2 us (99%)
    pallas_call x1, Pallas kernels, local(): pl.pallas_call(kernel, out_shape=tuple((pltpu.VMEM(a.shape, a.dtype) for...  70 us

profile of v5, /device:TPU:1, one launch (start us, length us, event | category | flops | bytes accessed | tf_op | source)
XLA Modules:
  0.0 71.8 jit_solution(11618243311477785104)
XLA Ops:
  0.6 70.0 %shard_map.77 = (f32[4,128,512]{2,1,0:T(8,128)S(1)}, f32[256,512]{1,0:T(8,128)S(1)}) custom-call(s32[8]{0:T(128)} %user_hbm.1, s32[8]{0:T(128)} %item_hbm.1, bf16[4,128,512]{2,1,0:T(8,128)(2,1)} %bitcast.3, bf16[2,2,64,512]{3,2,1,0:T(8,128)(2,1)} %bitcast.4, bf16[8,128,128]{2,1,0:T(8,128)(2,1)} %w_hbm.1, bf16[8,128,128]{2,1,0:T(8,128)(2,1)} %t_hbm.1), custom_call_target="tpu_custom_call" | custom-call | tf_op jit(solution)/shard_map/pallas_call | solution.py:293
  70.6 1.2 %shard_map.78 = (f32[4,128,512]{2,1,0:T(8,128)}, f32[256,512]{1,0:T(8,128)}) custom-call(f32[4,128,512]{2,1,0:T(8,128)S(1)} %get-tuple-element.6.ug, f32[256,512]{1,0:T(8,128)S(1)} %get-tuple-element.7.ig), custom_call_target="tpu_custom_call" | custom-call | tf_op jit(solution)/shard_map/pallas_call | solution.py:340
